TPU v7x, 256 devices: a whole 4x4x8 slice. The times are simulated.
256 devices in a mesh: tgt: 32 (over y, x, z_lo), src: 8 (over z_hi, core).
Axes of the slice: x: 4, y: 4, z: 8 (z_hi: 4, z_lo: 2; z = z_hi * 2 + z_lo), core: 2. Of those that a mesh axis runs over, the one named last changes fastest.
Arguments:
- connectome: bfloat16 [4096, 51200], P('tgt', 'src'), may hold values from -0.02734375 to 0.02734375
- history: bfloat16 [32, 32, 51200], P('tgt', None, 'src'), may hold values from 0 to 5
- delays: int32 [32, 400], P('tgt', 'src'), may hold values from 16 to 32
- cycle_head: int32 [1], replicated, may hold values from 0 to 31
- outside_afferent: float32 [32], replicated, may hold values from 120 to 320
- init_state: float32 [6, 32, 4096], P(None, None, 'tgt'), may hold values from -4 to 4
- lead_field: bfloat16 [4096, 256], P('tgt'), may hold values from -0.09375 to 0.09375
Outputs:
- sensor_signal: float32 [32, 16, 256], P('tgt')
- final_state: float32 [6, 32, 4096], P(None, None, ('tgt', 'src'))
Inputs may be any that keep to these rules, and one draw needn't show every extreme that they name: `cycle_head`: a slot of the history cycle.
All inputs are finite; a program needn't handle non-finite values.
Results may differ from a plain program's by a relative error of at most 0.003.
Values may be sent and summed in bfloat16 or wider, within the bound.
No kernel may reach another device: no remote copies, remote signals or barrier semaphores. Data moves between devices by JAX's collectives and lax.ppermute only.
A program may use at most 128 MiB of HBM per device.

v0:
```python
import jax
import jax.numpy as jnp
from jax import lax
from jax.sharding import PartitionSpec as P

STEPS = 16
integrator_step_width = 0.1
positive_synaptic_amplitude = 0.0325
negative_synaptic_amplitude = 0.11
interneuron_fraction = 0.5
global_link_scale = 30.0
stellate_contact_count = 135.0
recurrent_loop_contacts = 108.0
interneuron_contact_count = 33.75
peak_spike_rate = 5.0
logistic_slope_factor = 0.56
logistic_midpoint = 6.0


def spike_rate_response(cell_depolarization):
    return peak_spike_rate * jax.nn.sigmoid(
        logistic_slope_factor * (cell_depolarization - logistic_midpoint)
    )


def advance(carry, applied_stimulus, outside_afferent):
    (
        principal_cell_depolarization,
        stellate_mean_depolarization,
        interneuron_mean_depolarization,
        principal_cell_slope,
        excite_rate,
        interneuron_slope,
    ) = carry
    next_principal_cell_slope = principal_cell_slope + integrator_step_width * (
        positive_synaptic_amplitude
        * spike_rate_response(stellate_mean_depolarization - interneuron_mean_depolarization)
        - 2.0 * principal_cell_slope
        - principal_cell_depolarization
    )
    summed_afferent_rate = (
        outside_afferent[:, None]
        + recurrent_loop_contacts
        * spike_rate_response(stellate_contact_count * principal_cell_depolarization)
        + global_link_scale * applied_stimulus
    )
    new_excite_rate = excite_rate + integrator_step_width * (
        positive_synaptic_amplitude * summed_afferent_rate
        - 2.0 * excite_rate
        - stellate_mean_depolarization
    )
    next_interneuron_slope = interneuron_slope + integrator_step_width * (
        negative_synaptic_amplitude
        * interneuron_contact_count
        * spike_rate_response(interneuron_contact_count * principal_cell_depolarization)
        - 2.0 * interneuron_fraction * interneuron_slope
        - interneuron_fraction * interneuron_fraction * interneuron_mean_depolarization
    )
    return (
        principal_cell_depolarization + integrator_step_width * principal_cell_slope,
        stellate_mean_depolarization + integrator_step_width * excite_rate,
        interneuron_mean_depolarization + integrator_step_width * interneuron_slope,
        next_principal_cell_slope,
        new_excite_rate,
        next_interneuron_slope,
    )


def integrate(init_state, outside_afferent, coupling):

    def one_step(carry, applied_stimulus):
        fresh = advance(carry, applied_stimulus, outside_afferent)
        return (fresh, fresh[1] - fresh[2])

    begin = tuple((init_state[member] for member in range(6)))
    final, potentials = lax.scan(one_step, begin, coupling)
    return (jnp.stack(final), potentials)


def body(connectome, history, delays, cycle_head, outside_afferent, init_state, lead_field):
    tgt_rows = connectome.shape[0]
    target_blocks = delays.shape[0]
    source_blocks = delays.shape[1]
    block_rows = tgt_rows // target_blocks
    block_cols = connectome.shape[1] // source_blocks
    members = history.shape[1]
    slots_all = history.shape[0] * lax.axis_size("tgt")
    tiles = connectome.reshape(target_blocks, block_rows, source_blocks, block_cols)
    moments = jnp.arange(STEPS, dtype=jnp.int32)
    lag_slot = (cycle_head[0] + moments[None, None, :] - delays[:, :, None]) % slots_all
    whole = lax.all_gather(history, "tgt", axis=0, tiled=True)
    stacked = whole.reshape(slots_all, members, source_blocks, block_cols)
    slot_ids = jnp.arange(slots_all, dtype=jnp.int32)
    wanted = lag_slot[0].T
    picker = (wanted[:, None, :] == slot_ids[None, :, None]).astype(jnp.bfloat16)
    window = jnp.einsum(
        "tkb,kmbs->tmbs", picker, stacked, preferred_element_type=jnp.float32
    ).astype(jnp.bfloat16)
    pieces = jnp.einsum("rbs,tmbs->tmr", tiles[0], window, preferred_element_type=jnp.float32)
    share = tgt_rows // lax.axis_size("src")
    offset_rows = lax.axis_index("src") * share
    summed = lax.psum(pieces, "src")
    final_full, potentials = integrate(init_state, outside_afferent, summed)
    final_state = lax.dynamic_slice_in_dim(final_full, offset_rows, share, 2)
    potential = potentials.astype(jnp.bfloat16)
    signal = lax.psum_scatter(
        jnp.einsum("tmr,rs->mts", potential, lead_field, preferred_element_type=jnp.float32),
        "tgt",
        scatter_dimension=0,
        tiled=True,
    )
    return (signal, final_state)


def solution(mesh):
    in_specs = (
        P("tgt", "src"),
        P("tgt", None, "src"),
        P("tgt", "src"),
        P(),
        P(),
        P(None, None, "tgt"),
        P("tgt", None),
    )
    out_specs = (P("tgt", None, None), P(None, None, ("tgt", "src")))
    return jax.shard_map(body, mesh=mesh, in_specs=in_specs, out_specs=out_specs, check_vma=False)
```

profile of v0, /device:TPU:64, one launch (start us, length us, event | category | flops | bytes accessed | tf_op | source)
XLA Modules:
  0.0 601.3 jit_solution(12034502340109940469)
XLA Ops:
  8.0 2.9 copy.27
  12.3 290.1 %all-gather.2.cloned.1.call-done = bf16[32,32,6400]{2,1,0:T(8,128)(2,1)} async-done(((bf16[1,32,6400]{2,1,0:T(8,128)(2,1)}), bf16[32,32,6400]{2,1,0:T(8,128)(2,1)}) %all-gather.2.cloned.1.call-update) | async-done | bytes 13107216 | tf_op jit(solution)/shard_map/all_gather | solution.py:91
  302.3 21.3 %reshape.45 = bf16[32,32,50,128]{3,2,1,0:T(8,128)(2,1)} reshape(bf16[32,32,6400]{2,1,0:T(8,128)(2,1)} %all-gather.2.cloned.1.call-done) | data formatting | bytes 26214400 | tf_op jit(solution)/shard_map/reshape | solution.py:92
  323.6 23.8 %fusion.10 = f32[16,32,128,1]{2,0,1,3:T(8,128)S(1)} fusion(bf16[128,50,128,1]{0,2,3,1:T(8,128)(2,1)S(1)} %bitcast.67, bf16[32,32,50,128]{3,2,1,0:T(8,128)(2,1)} %reshape.45, s32[16,50]{0,1:T(8,128)S(1)} %add_select_fusion), kind=kOutput, calls=%fused_computation.15 | convolution fusion | flops 1051878400 | bytes 15010944 | tf_op jit(solution)/shard_map/rbs,tmbs->tmr/dot_general | solution.py:99
  348.3 67.0 %all-reduce.2.cloned.1.call-done = f32[16,32,128]{2,1,0:T(8,128)} async-done(((f32[16,32,128]{2,1,0:T(8,128)}), f32[16,32,128]{2,1,0:T(8,128)}) %all-reduce.2.cloned.1.call-update) | async-done | bytes 262160 | tf_op jit(solution)/shard_map/psum | solution.py:102
  415.3 13.6 %while.25 = (s32[]{:T(128)}, f32[32,128]{1,0:T(8,128)S(1)}, f32[32,128]{1,0:T(8,128)S(1)}, f32[32,128]{1,0:T(8,128)S(1)}, f32[32,128]{1,0:T(8,128)S(1)}, /*index...) while((s32[]{:T(128)}, f32[32,128]{1,0:T(8,128)S(1)}, ...), condition=%wide.region_2.3_spmd, body=%wide.region_1.2_spmd.sunk | while | flops 192514 | bytes 360693 | solution.py:76
  415.3 0.8 multiply_add_fusion.8
  416.2 0.8 multiply_add_fusion.8
  417.0 0.8 multiply_add_fusion.8
  417.9 0.8 multiply_add_fusion.8
  418.7 0.8 multiply_add_fusion.8
  419.6 0.8 multiply_add_fusion.8
  420.4 0.8 multiply_add_fusion.8
  421.3 0.8 multiply_add_fusion.8
  422.1 0.8 multiply_add_fusion.8
  423.0 0.8 multiply_add_fusion.8
  423.8 0.8 multiply_add_fusion.8
  424.7 0.8 multiply_add_fusion.8
  425.5 0.8 multiply_add_fusion.8
  426.4 0.8 multiply_add_fusion.8
  427.2 0.8 multiply_add_fusion.8
  428.1 0.8 multiply_add_fusion.8
  429.2 1.1 copy.30
  431.2 163.6 %reduce-scatter.2.cloned.1.call-done = f32[1,16,256]{2,1,0:T(8,128)} async-done(((f32[32,16,256]{2,1,0:T(8,128)}), f32[1,16,256]{2,1,0:T(8,128)}) %reduce-scatter.2.cloned.1.call-update) | async-done | bytes 16400 | tf_op jit(solution)/shard_map/reduce_scatter | solution.py:106
  (74 shorter events, 3.8 us)
Async XLA Ops:
  7.2 421.8 %copy-start = (bf16[128,256]{1,0:T(8,128)(2,1)S(1)}, bf16[128,256]{1,0:T(8,128)(2,1)}, u32[]{:S(2)}) copy-start(bf16[128,256]{1,0:T(8,128)(2,1)} %param.15) | copy-start | bytes 196612
  7.2 295.2 %all-gather.2.cloned.1.call-start = ((), (), s32[]{:S(2)}) async-start(), calls=%async_computation.1 | async-start | bytes 13516800 | tf_op jit(solution)/shard_map/all_gather | solution.py:91
  7.9 407.4 %all-reduce.2.cloned.1.call-start = ((), (), s32[]{:S(2)}) async-start(), calls=%async_computation.2 | async-start | bytes 524288 | tf_op jit(solution)/shard_map/psum | solution.py:102
  323.6 24.7 %copy-start.1 = (f32[6,32,128]{2,1,0:T(8,128)S(1)}, f32[6,32,128]{2,1,0:T(8,128)}, u32[]{:S(2)}) copy-start(f32[6,32,128]{2,1,0:T(8,128)} %param.14) | copy-start | bytes 294916
  323.6 91.7 %copy-start.2 = (f32[32]{0:T(128)S(1)}, f32[32]{0:T(128)}, u32[]{:S(2)}) copy-start(f32[32]{0:T(128)} %param.13) | copy-start | bytes 388
  348.2 246.6 %reduce-scatter.2.cloned.1.call-start = ((), (), s32[]{:S(2)}) async-start(), calls=%async_computation.3 | async-start | bytes 540672 | tf_op jit(solution)/shard_map/reduce_scatter | solution.py:106
Sparse Core Ops, SparseCore 0:
  9.8 292.4 all-gather.1
  348.3 66.9 all-reduce.1
  430.4 164.3 reduce-scatter.1
where the time goes:
time: 603 us; the launch traced here: 601 us
  waiting for transfers between devices  521 us (86%)
  local copies, waits for them, and re-layouts  27 us (4%)
  matrix products  24 us (4%)
  between operations  14.5 us (2%)
  other arithmetic  13.7 us (2%)
    all_gather x1, waiting for transfers between devices, body(): whole = lax.all_gather(history, 'tgt', axis=0, tiled=True)  290 us
    reduce_scatter x1, waiting for transfers between devices, body(): lax.psum_scatter(jnp.einsum('tmr,rs->mts', potential, lead_field, preferr...  164 us
    psum x1, waiting for transfers between devices, body(): summed = lax.psum(pieces, 'src')  67 us
    dot_general x1, matrix products, body(): jnp.einsum('rbs,tmbs->tmr', tiles[0], window, preferred_element_type=jnp....  23.8 us
    reshape x1, local copies, waits for them, and re-layouts, body(): stacked = whole.reshape(slots_all, members, source_blocks, block_cols)  21.3 us
    add x16, other arithmetic, advance(): interneuron_slope + integrator_step_width * (negative_synaptic_amplitude...  12.7 us
  transfers between devices with their start and end apart: 3, of which 3 were waited for; matrix products, arithmetic and copies ran while one was open for 1% of the time, Pallas kernels for 0%

commit v1 on v0

--- a/solution.py
+++ b/solution.py
@@ -88,7 +88,9 @@
     tiles = connectome.reshape(target_blocks, block_rows, source_blocks, block_cols)
     moments = jnp.arange(STEPS, dtype=jnp.int32)
     lag_slot = (cycle_head[0] + moments[None, None, :] - delays[:, :, None]) % slots_all
-    whole = lax.all_gather(history, "tgt", axis=0, tiled=True)
+    whole = jnp.concatenate(
+        lax.all_to_all(jnp.stack([history] * lax.axis_size("tgt")), "tgt", 0, 0), axis=0
+    )
     stacked = whole.reshape(slots_all, members, source_blocks, block_cols)
     slot_ids = jnp.arange(slots_all, dtype=jnp.int32)
     wanted = lag_slot[0].T

time: 603 us -> 545 us (0.904)
  waiting for transfers between devices: 521 us -> 449 us
  starting transfers between devices: 0.12 us -> 9 us
    all_gather x1 -> x0, waiting for transfers between devices: 290 us -> none  [body(): whole = lax.all_gather(history, 'tgt', axis=0, tiled=True)]
    all_to_all x0 -> x1, waiting for transfers between devices: none -> 190 us  [body(): lax.all_to_all(jnp.stack([history] * lax.axis_size('tgt')), 'tgt', 0, 0)]
    psum x1, waiting for transfers between devices: 67 us -> 95.6 us  [body(): summed = lax.psum(pieces, 'src')]
    another operation x0 -> x2, local copies, waits for them, and re-layouts: none -> 28.5 us  [the longest x1 21.3 us: body(): stacked = whole.reshape(slots_all, members, source_blocks, block_cols)]
    reshape x1 -> x0, local copies, waits for them, and re-layouts: 21.3 us -> none  [body(): stacked = whole.reshape(slots_all, members, source_blocks, block_cols)]
    all_to_all x0 -> x1, starting transfers between devices: none -> 8.92 us  [body(): lax.all_to_all(jnp.stack([history] * lax.axis_size('tgt')), 'tgt', 0, 0)]
  transfers between devices with their start and end apart: 3 -> 3, of which waited for: 3 -> 3; matrix products, arithmetic and copies ran while one was open for 1% -> 0% of each run, Pallas kernels for 0% -> 0%
where the time goes in v1:
time: 545 us; the launch traced here: 543 us
  waiting for transfers between devices  449 us (82%)
  local copies, waits for them, and re-layouts  32.8 us (6%)
  matrix products  24 us (4%)
  between operations  14.9 us (3%)
  other arithmetic  13.1 us (2%)
  starting transfers between devices  9 us (2%)
    all_to_all x1, waiting for transfers between devices, body(): lax.all_to_all(jnp.stack([history] * lax.axis_size('tgt')), 'tgt', 0, 0)  190 us
    reduce_scatter x1, waiting for transfers between devices, body(): lax.psum_scatter(jnp.einsum('tmr,rs->mts', potential, lead_field, preferr...  163 us
    psum x1, waiting for transfers between devices, body(): summed = lax.psum(pieces, 'src')  95.6 us
    dot_general x1, matrix products, body(): jnp.einsum('rbs,tmbs->tmr', tiles[0], window, preferred_element_type=jnp....  23.8 us
    another operation x1, local copies, waits for them, and re-layouts, body(): stacked = whole.reshape(slots_all, members, source_blocks, block_cols)  21.3 us
    add x16, other arithmetic, advance(): interneuron_slope + integrator_step_width * (negative_synaptic_amplitude...  12.7 us
  transfers between devices with their start and end apart: 3, of which 3 were waited for; matrix products, arithmetic and copies ran while one was open for 0% of the time, Pallas kernels for 0%

profile of v1, /device:TPU:64, one launch (start us, length us, event | category | flops | bytes accessed | tf_op | source)
XLA Modules:
  0.0 542.9 jit_solution(8627449223464097939)
XLA Ops:
  7.2 7.2 %stack.16 = bf16[32,1,32,6400]{3,2,1,0:T(8,128)(2,1)} broadcast(bf16[32,6400]{1,0:T(8,128)(2,1)} %bitcast.72), dimensions={2,3} | broadcast | bytes 13516800 | tf_op jit(solution)/shard_map/stack | solution.py:92
  14.4 8.9 %all-to-all-start = ((bf16[32,1,32,6400]{3,2,1,0:T(8,128)(2,1)}), bf16[32,1,32,6400]{3,2,1,0:T(8,128)(2,1)}, u32[]{:S(2)}, u32[]{:S(2)}) async-start(bf16[32,1,32,6400]{3,2,1,0:T(8,128)(2,1)} %stack.16), calls=%async_computation | async-start | bytes 26214400 | tf_op jit(solution)/shard_map/all_to_all | solution.py:92
  23.4 1.5 copy.27
  25.6 189.7 %all-to-all-done = bf16[32,1,32,6400]{3,2,1,0:T(8,128)(2,1)} async-done(((bf16[32,1,32,6400]{3,2,1,0:T(8,128)(2,1)}), bf16[32,1,32,6400]{3,2,1,0:T(8,128)(2,1)}, u32[]{:S(2)}, u32[]{:S(2)}) %all-to-all-start) | async-done | bytes 13107232 | tf_op jit(solution)/shard_map/all_to_all | solution.py:92
  215.3 21.3 %reshape_reshape.3 = bf16[32,32,50,128]{3,2,1,0:T(8,128)(2,1)} reshape(bf16[32,1,32,6400]{3,2,1,0:T(8,128)(2,1)} %all-to-all-done) | data formatting | bytes 26214400 | tf_op jit(solution)/shard_map/reshape;reshape | solution.py:94
  236.6 23.8 %fusion.10 = f32[16,32,128,1]{2,0,1,3:T(8,128)S(1)} fusion(bf16[128,50,128,1]{0,2,3,1:T(8,128)(2,1)S(1)} %bitcast.70, bf16[32,32,50,128]{3,2,1,0:T(8,128)(2,1)} %reshape_reshape.3, s32[16,50]{0,1:T(8,128)S(1)} %add_select_fusion), kind=kOutput, calls=%fused_computation.15 | convolution fusion | flops 1051878400 | bytes 15010944 | tf_op jit(solution)/shard_map/rbs,tmbs->tmr/dot_general | solution.py:101
  261.3 95.6 %all-reduce.2.cloned.1.call-done = f32[16,32,128]{2,1,0:T(8,128)} async-done(((f32[16,32,128]{2,1,0:T(8,128)}), f32[16,32,128]{2,1,0:T(8,128)}) %all-reduce.2.cloned.1.call-update) | async-done | bytes 262160 | tf_op jit(solution)/shard_map/psum | solution.py:104
  356.9 13.6 %while.25 = (s32[]{:T(128)}, f32[32,128]{1,0:T(8,128)S(1)}, f32[32,128]{1,0:T(8,128)S(1)}, f32[32,128]{1,0:T(8,128)S(1)}, f32[32,128]{1,0:T(8,128)S(1)}, /*index...) while((s32[]{:T(128)}, f32[32,128]{1,0:T(8,128)S(1)}, ...), condition=%wide.region_2.3_spmd, body=%wide.region_1.2_spmd.sunk | while | flops 192514 | bytes 360693 | solution.py:76
  357.8 0.8 multiply_add_fusion.8
  358.6 0.8 multiply_add_fusion.8
  359.5 0.8 multiply_add_fusion.8
  360.3 0.8 multiply_add_fusion.8
  361.2 0.8 multiply_add_fusion.8
  362.0 0.8 multiply_add_fusion.8
  362.9 0.8 multiply_add_fusion.8
  363.7 0.8 multiply_add_fusion.8
  364.6 0.8 multiply_add_fusion.8
  365.4 0.8 multiply_add_fusion.8
  366.3 0.8 multiply_add_fusion.8
  367.1 0.8 multiply_add_fusion.8
  368.0 0.8 multiply_add_fusion.8
  369.7 0.8 multiply_add_fusion.8
  370.8 1.1 copy.30
  372.8 163.3 %reduce-scatter.2.cloned.1.call-done = f32[1,16,256]{2,1,0:T(8,128)} async-done(((f32[32,16,256]{2,1,0:T(8,128)}), f32[1,16,256]{2,1,0:T(8,128)}) %reduce-scatter.2.cloned.1.call-update) | async-done | bytes 16400 | tf_op jit(solution)/shard_map/reduce_scatter | solution.py:108
  (78 shorter events, 4.0 us)
Async XLA Ops:
  7.2 363.4 %copy-start = (bf16[128,256]{1,0:T(8,128)(2,1)S(1)}, bf16[128,256]{1,0:T(8,128)(2,1)}, u32[]{:S(2)}) copy-start(bf16[128,256]{1,0:T(8,128)(2,1)} %param.15) | copy-start | bytes 196612
  14.4 9.0 %copy-start.1 = (bf16[128,6400]{1,0:T(8,128)(2,1)S(1)}, bf16[128,6400]{1,0:T(8,128)(2,1)}, u32[]{:S(2)}) copy-start(bf16[128,6400]{1,0:T(8,128)(2,1)} %param.9) | copy-start | bytes 4915204
  14.4 11.1 %copy-start.4 = (s32[1,50]{1,0:T(1,128)S(1)}, s32[1,50]{1,0:T(1,128)}, u32[]{:S(2)}) copy-start(s32[1,50]{1,0:T(1,128)} %param.11) | copy-start | bytes 604
  14.4 200.9 %all-to-all-start = ((bf16[32,1,32,6400]{3,2,1,0:T(8,128)(2,1)}), bf16[32,1,32,6400]{3,2,1,0:T(8,128)(2,1)}, u32[]{:S(2)}, u32[]{:S(2)}) async-start(bf16[32,1,32,6400]{3,2,1,0:T(8,128)(2,1)} %stack.16), calls=%async_computation | async-start | bytes 26214400 | tf_op jit(solution)/shard_map/all_to_all | solution.py:92
  23.3 333.6 %all-reduce.2.cloned.1.call-start = ((), (), s32[]{:S(2)}) async-start(), calls=%async_computation.2 | async-start | bytes 524288 | tf_op jit(solution)/shard_map/psum | solution.py:104
  236.6 24.7 %copy-start.2 = (f32[6,32,128]{2,1,0:T(8,128)S(1)}, f32[6,32,128]{2,1,0:T(8,128)}, u32[]{:S(2)}) copy-start(f32[6,32,128]{2,1,0:T(8,128)} %param.14) | copy-start | bytes 294916
  236.6 120.3 %copy-start.3 = (f32[32]{0:T(128)S(1)}, f32[32]{0:T(128)}, u32[]{:S(2)}) copy-start(f32[32]{0:T(128)} %param.13) | copy-start | bytes 388
  261.2 274.9 %reduce-scatter.2.cloned.1.call-start = ((), (), s32[]{:S(2)}) async-start(), calls=%async_computation.3 | async-start | bytes 540672 | tf_op jit(solution)/shard_map/reduce_scatter | solution.py:108
Sparse Core Ops, SparseCore 0:
  261.3 95.5 all-reduce.1
  372.0 163.9 reduce-scatter.1

commit v2 on v0

--- a/solution.py
+++ b/solution.py
@@ -99,7 +99,7 @@
     pieces = jnp.einsum("rbs,tmbs->tmr", tiles[0], window, preferred_element_type=jnp.float32)
     share = tgt_rows // lax.axis_size("src")
     offset_rows = lax.axis_index("src") * share
-    summed = lax.psum(pieces, "src")
+    summed = jnp.sum(lax.all_gather(pieces, "src"), axis=0)
     final_full, potentials = integrate(init_state, outside_afferent, summed)
     final_state = lax.dynamic_slice_in_dim(final_full, offset_rows, share, 2)
     potential = potentials.astype(jnp.bfloat16)

time: 603 us -> 556 us (0.922)
  waiting for transfers between devices: 521 us -> 485 us
  other arithmetic: 13.7 us -> 4.03 us
    psum x1 -> x0, waiting for transfers between devices: 67 us -> none  [body(): summed = lax.psum(pieces, 'src')]
    all_gather x0 -> x1, waiting for transfers between devices: none -> 33 us  [body(): summed = jnp.sum(lax.all_gather(pieces, 'src'), axis=0)]
    add x16, other arithmetic: 12.7 us -> 1.19 us  [advance(): interneuron_slope + integrator_step_width * (negative_synaptic_amplitude...]
where the time goes in v2:
time: 556 us; the launch traced here: 555 us
  waiting for transfers between devices  485 us (87%)
  local copies, waits for them, and re-layouts  27 us (5%)
  matrix products  24 us (4%)
  between operations  14.5 us (3%)
    all_gather x1, waiting for transfers between devices, body(): whole = lax.all_gather(history, 'tgt', axis=0, tiled=True)  290 us
    reduce_scatter x1, waiting for transfers between devices, body(): lax.psum_scatter(jnp.einsum('tmr,rs->mts', potential, lead_field, preferr...  161 us
    all_gather x1, waiting for transfers between devices, body(): summed = jnp.sum(lax.all_gather(pieces, 'src'), axis=0)  33 us
    dot_general x1, matrix products, body(): jnp.einsum('rbs,tmbs->tmr', tiles[0], window, preferred_element_type=jnp....  23.8 us
    reshape x1, local copies, waits for them, and re-layouts, body(): stacked = whole.reshape(slots_all, members, source_blocks, block_cols)  21.3 us
  transfers between devices with their start and end apart: 3, of which 3 were waited for; matrix products, arithmetic and copies ran while one was open for 1% of the time, Pallas kernels for 0%

profile of v2, /device:TPU:64, one launch (start us, length us, event | category | flops | bytes accessed | tf_op | source)
XLA Modules:
  0.0 554.9 jit_solution(1225852157315472453)
XLA Ops:
  7.2 0.7 all-gather.4.cloned.1.call-update
  8.0 2.9 copy.27
  11.5 0.7 add_select_fusion
  12.3 290.1 %all-gather.4.cloned.1.call-done = bf16[32,32,6400]{2,1,0:T(8,128)(2,1)} async-done(((bf16[1,32,6400]{2,1,0:T(8,128)(2,1)}), bf16[32,32,6400]{2,1,0:T(8,128)(2,1)}) %all-gather.4.cloned.1.call-update) | async-done | bytes 13107216 | tf_op jit(solution)/shard_map/all_gather | solution.py:91
  302.3 21.3 %reshape.45 = bf16[32,32,50,128]{3,2,1,0:T(8,128)(2,1)} reshape(bf16[32,32,6400]{2,1,0:T(8,128)(2,1)} %all-gather.4.cloned.1.call-done) | data formatting | bytes 26214400 | tf_op jit(solution)/shard_map/reshape | solution.py:92
  323.6 23.8 %fusion.10 = f32[16,32,128,1]{2,0,1,3:T(8,128)S(1)} fusion(bf16[128,50,128,1]{0,2,3,1:T(8,128)(2,1)S(1)} %bitcast.69, bf16[32,32,50,128]{3,2,1,0:T(8,128)(2,1)} %reshape.45, s32[16,50]{0,1:T(8,128)S(1)} %add_select_fusion), kind=kOutput, calls=%fused_computation.15 | convolution fusion | flops 1051878400 | bytes 15010944 | tf_op jit(solution)/shard_map/rbs,tmbs->tmr/dot_general | solution.py:99
  347.4 0.8 copy.47
  348.3 33.0 %all-gather.6.cloned.1.call-done = f32[128,32,128]{2,1,0:T(8,128)} async-done(((f32[16,32,128]{2,1,0:T(8,128)}), f32[128,32,128]{2,1,0:T(8,128)}) %all-gather.6.cloned.1.call-update) | async-done | bytes 2097168 | tf_op jit(solution)/shard_map/all_gather | solution.py:102
  381.3 1.8 reduce_sum.9
  383.2 2.1 while.25
  383.2 0.1 multiply_add_fusion.8
  383.3 0.1 multiply_add_fusion.8
  383.6 0.1 multiply_add_fusion.8
  383.7 0.1 multiply_add_fusion.8
  384.0 0.1 multiply_add_fusion.8
  384.2 0.1 multiply_add_fusion.8
  384.5 0.1 multiply_add_fusion.8
  384.8 0.1 multiply_add_fusion.8
  385.1 0.1 multiply_add_fusion.8
  385.3 0.2 convolution_bitcast_fusion
  385.5 1.1 copy.30
  386.7 0.1 constant_dynamic-slice_fusion
  386.8 0.7 copy.31
  387.5 160.8 %reduce-scatter.2.cloned.1.call-done = f32[1,16,256]{2,1,0:T(8,128)} async-done(((f32[32,16,256]{2,1,0:T(8,128)}), f32[1,16,256]{2,1,0:T(8,128)}) %reduce-scatter.2.cloned.1.call-update) | async-done | bytes 16400 | tf_op jit(solution)/shard_map/reduce_scatter | solution.py:106
  (75 shorter events, 1.1 us)
Async XLA Ops:
  7.2 378.2 %copy-start = (bf16[128,256]{1,0:T(8,128)(2,1)S(1)}, bf16[128,256]{1,0:T(8,128)(2,1)}, u32[]{:S(2)}) copy-start(bf16[128,256]{1,0:T(8,128)(2,1)} %param.15) | copy-start | bytes 196612
  7.2 295.2 %all-gather.4.cloned.1.call-start = ((), (), s32[]{:S(2)}) async-start(), calls=%async_computation.1 | async-start | bytes 13516800 | tf_op jit(solution)/shard_map/all_gather | solution.py:91
  7.9 373.4 %all-gather.6.cloned.1.call-start = ((), (), s32[]{:S(2)}) async-start(), calls=%async_computation.3 | async-start | bytes 2359296 | tf_op jit(solution)/shard_map/all_gather | solution.py:102
  323.6 24.7 %copy-start.1 = (f32[6,32,128]{2,1,0:T(8,128)S(1)}, f32[6,32,128]{2,1,0:T(8,128)}, u32[]{:S(2)}) copy-start(f32[6,32,128]{2,1,0:T(8,128)} %param.14) | copy-start | bytes 294916
  323.6 59.5 %copy-start.2 = (f32[32]{0:T(128)S(1)}, f32[32]{0:T(128)}, u32[]{:S(2)}) copy-start(f32[32]{0:T(128)} %param.13) | copy-start | bytes 388
  348.2 200.1 %reduce-scatter.2.cloned.1.call-start = ((), (), s32[]{:S(2)}) async-start(), calls=%async_computation.2 | async-start | bytes 540672 | tf_op jit(solution)/shard_map/reduce_scatter | solution.py:106
Sparse Core Ops, SparseCore 0:
  9.8 292.4 all-gather.3
  348.3 32.9 all-gather.5
  386.8 161.5 reduce-scatter.1
